TPU v7x, 32 devices: a whole 2x2x4 slice. The times are simulated.
32 devices in a mesh: rows: 8 (over z, y), band: 4 (over x, core).
Axes of the slice: x: 2, y: 2, z: 4, core: 2. Of those that a mesh axis runs over, the one named last changes fastest.
Arguments:
- embedding: bfloat16 [1024, 512], P('rows'), may hold values from -6 to 6
- w_left: bfloat16 [512, 32], replicated, may hold values from -0.25 to 0.25
- w_right: bfloat16 [512, 32], replicated, may hold values from -0.25 to 0.25
- w_in: bfloat16 [32, 128], replicated, may hold values from -1 to 1
- w_out: bfloat16 [128, 32], replicated, may hold values from -0.5 to 0.5
- w_head: float32 [32], replicated, may hold values from -1 to 1
- dist_bias: float32 [32, 4], replicated, may hold values from -3 to 3
- offsets: int32 [8, 4], P('rows', 'band'), may hold values from 0 to 3, each once within a row
- valid_bins: int32 [1024], P('rows'), may hold values 0 or 1
- target: bfloat16 [8, 4, 128, 128], P('rows', 'band'), may hold values from -6 to 6
Outputs:
- predicted: bfloat16 [8, 4, 128, 128], P('rows', 'band')
- grad_embedding: bfloat16 [1024, 512], P('rows', 'band')
- grad_left: float32 [512, 32], replicated
- grad_right: float32 [512, 32], replicated
- grad_in: float32 [32, 128], replicated
- grad_out: float32 [128, 32], replicated
- grad_head: float32 [32], replicated
- grad_bias: float32 [32, 4], replicated
Inputs may be any that keep to these rules, and one draw needn't show every extreme that they name: `offsets`: each row tile's 4 entries are the numbers 0 to 3 in some order.
All inputs are finite; a program needn't handle non-finite values. No bound on the sum of `valid_bins` on one device may be relied on, other than what follows from the above.
Results may differ from a plain program's by a relative error of at most 0.0058.
Values may be sent and summed in bfloat16 or wider, within the bound.
No kernel may reach another device: no remote copies, remote signals or barrier semaphores. Data moves between devices by JAX's collectives and lax.ppermute only.
A program may use at most 64 MiB of HBM per device.

v0:
```python
import jax
import jax.numpy as jnp
from jax import lax
from jax.sharding import PartitionSpec as P

TILE = 128
NOFF = 4


def from_behind(value, axis, steps):
    count = lax.axis_size(axis)
    leading, last = (max(0, -steps), min(count, count - steps))
    return lax.ppermute(value, axis, [(source, source + steps) for source in range(leading, last)])


def gelu_pair(pre_act):
    return jax.nn.gelu(pre_act, approximate=True)


def block_terms(row_proj, col_proj, bias_col, row_flags, col_flags, goal_rows, w_in, w_out, w_head):
    channels = row_proj.shape[0]
    row_count = row_proj.shape[1]
    col_count = col_proj.shape[1]
    summed = (
        row_proj.astype(jnp.float32)[:, :, None]
        + col_proj.astype(jnp.float32)[:, None, :]
        + bias_col[:, None, None]
    )
    summed = summed.reshape(channels, row_count * col_count)
    pair_in = summed.astype(jnp.bfloat16)
    pre_act = lax.dot_general(
        w_in, pair_in, (((0,), (0,)), ((), ())), preferred_element_type=jnp.float32
    )
    activation = gelu_pair(pre_act).astype(jnp.bfloat16)
    update = summed + lax.dot_general(
        w_out, activation, (((0,), (0,)), ((), ())), preferred_element_type=jnp.float32
    )
    logits = jnp.dot(w_head, update, precision=lax.Precision.HIGHEST)
    weight_mask = (row_flags[:, None] * col_flags[None, :]).reshape(-1)
    residual = weight_mask * (logits - goal_rows.astype(jnp.float32).reshape(-1)) / (NOFF * TILE)
    grad_update = w_head[:, None] * residual[None, :]
    grad_low = grad_update.astype(jnp.bfloat16)
    head_term = jnp.dot(update, residual, precision=lax.Precision.HIGHEST)
    out_term = lax.dot_general(
        activation, grad_low, (((1,), (1,)), ((), ())), preferred_element_type=jnp.float32
    )
    grad_act = lax.dot_general(
        w_out, grad_low, (((1,), (0,)), ((), ())), preferred_element_type=jnp.float32
    )
    _, backward = jax.vjp(gelu_pair, pre_act)
    grad_pre = backward(grad_act)[0].astype(jnp.bfloat16)
    in_term = lax.dot_general(
        pair_in, grad_pre, (((1,), (1,)), ((), ())), preferred_element_type=jnp.float32
    )
    grad_pair = grad_update + lax.dot_general(
        w_in, grad_pre, (((1,), (0,)), ((), ())), preferred_element_type=jnp.float32
    )
    grad_cube = grad_pair.reshape(channels, row_count, col_count)
    return (
        logits.reshape(row_count, col_count),
        head_term,
        out_term,
        in_term,
        jnp.sum(grad_pair, axis=1),
        jnp.sum(grad_cube, axis=2),
        jnp.sum(grad_cube, axis=1),
    )


def tile_terms(row_proj, col_proj, bias_col, row_flags, col_flags, goal_tile, w_in, w_out, w_head):
    half_rows = row_proj.shape[1] // 2
    first = block_terms(
        row_proj[:, :half_rows],
        col_proj,
        bias_col,
        row_flags[:half_rows],
        col_flags,
        goal_tile[:half_rows],
        w_in,
        w_out,
        w_head,
    )
    second = block_terms(
        row_proj[:, half_rows:],
        col_proj,
        bias_col,
        row_flags[half_rows:],
        col_flags,
        goal_tile[half_rows:],
        w_in,
        w_out,
        w_head,
    )
    return (
        jnp.concatenate([first[0], second[0]], axis=0),
        first[1] + second[1],
        first[2] + second[2],
        first[3] + second[3],
        first[4] + second[4],
        jnp.concatenate([first[5], second[5]], axis=1),
        first[6] + second[6],
    )


def project(embedding, weight):
    return lax.dot_general(
        weight, embedding, (((0,), (1,)), ((), ())), preferred_element_type=jnp.float32
    ).astype(jnp.bfloat16)


def fetch_ahead(right_proj, flags_low, step_count):
    return from_behind((right_proj, flags_low), "rows", -step_count)


def return_behind(col_piece, step_count):
    return from_behind(col_piece, "rows", step_count)


def on_device(
    embedding, w_left, w_right, w_in, w_out, w_head, dist_bias, offsets, valid_bins, target
):
    bin_count = embedding.shape[0]
    tile_count = bin_count // TILE
    slot_count = offsets.shape[1]
    reach_count = (NOFF + tile_count - 2) // tile_count
    channels = w_left.shape[1]
    hidden = w_in.shape[1]
    left_proj = project(embedding, w_left)
    right_proj = project(embedding, w_right)
    flags_low = valid_bins.astype(jnp.bfloat16)
    proj_parts = [right_proj]
    flag_parts = [flags_low]
    for step_count in range(1, reach_count + 1):
        moved_proj, moved_flags = fetch_ahead(right_proj, flags_low, step_count)
        proj_parts.append(moved_proj)
        flag_parts.append(moved_flags)
    right_ext = jnp.concatenate(proj_parts, axis=1)
    flags_ext = jnp.concatenate(flag_parts, axis=0).astype(jnp.float32)
    extended = bin_count * (reach_count + 1)
    initial = (
        jnp.zeros((channels, bin_count), jnp.float32),
        jnp.zeros((channels, extended), jnp.float32),
        jnp.zeros((channels, hidden), jnp.float32),
        jnp.zeros((hidden, channels), jnp.float32),
        jnp.zeros((channels,), jnp.float32),
        jnp.zeros((channels, NOFF), jnp.float32),
    )

    def advance(totals, item_index):
        tile_row = item_index // slot_count
        slot_index = item_index % slot_count
        offset = offsets[tile_row, slot_index]
        one_hot = (jnp.arange(NOFF, dtype=jnp.int32) == offset).astype(jnp.float32)
        bias_col = jnp.sum(dist_bias * one_hot[None, :], axis=1)
        row_start = tile_row * TILE
        col_start = (tile_row + offset) * TILE
        col_proj = lax.dynamic_slice_in_dim(right_ext, col_start, TILE, 1)
        row_flags = lax.dynamic_slice_in_dim(flags_ext, row_start, TILE, 0)
        col_flags = lax.dynamic_slice_in_dim(flags_ext, col_start, TILE, 0)
        goal_tile = target[tile_row, slot_index]
        logits, head_term, out_term, in_term, bias_sum, row_sums, col_sums = tile_terms(
            left_proj, col_proj, bias_col, row_flags, col_flags, goal_tile, w_in, w_out, w_head
        )
        row_acc, col_acc, in_acc, out_acc, head_acc, bias_acc = totals
        row_acc = row_acc + row_sums
        col_acc = lax.dynamic_update_slice_in_dim(
            col_acc, lax.dynamic_slice_in_dim(col_acc, col_start, TILE, 1) + col_sums, col_start, 1
        )
        bias_acc = bias_acc + bias_sum[:, None] * one_hot[None, :]
        return (
            (
                row_acc,
                col_acc,
                in_acc + in_term,
                out_acc + out_term,
                head_acc + head_term,
                bias_acc,
            ),
            logits,
        )

    totals, logits = lax.scan(
        advance, initial, jnp.arange(tile_count * slot_count, dtype=jnp.int32)
    )
    row_acc, col_acc, in_part, out_part, head_part, bias_part = totals
    predicted = logits.reshape(tile_count, slot_count, TILE, TILE).astype(jnp.bfloat16)
    col_own = col_acc[:, :bin_count]
    for step_count in range(1, reach_count + 1):
        col_piece = col_acc[:, step_count * bin_count : (step_count + 1) * bin_count]
        col_own = col_own + return_behind(col_piece, step_count)
    row_total, col_total = lax.psum((row_acc, col_own), "band")
    row_grad = row_total.astype(jnp.bfloat16)
    col_grad = col_total.astype(jnp.bfloat16)
    grad_in, grad_out, grad_head, grad_bias = lax.psum(
        (in_part, out_part, head_part, bias_part), ("rows", "band")
    )
    share = embedding.shape[1] // lax.axis_size("band")
    share_start = lax.axis_index("band") * share
    left_share = lax.dynamic_slice_in_dim(w_left, share_start, share, 0)
    right_share = lax.dynamic_slice_in_dim(w_right, share_start, share, 0)
    grad_embedding = (
        lax.dot_general(
            row_grad, left_share, (((0,), (1,)), ((), ())), preferred_element_type=jnp.float32
        )
        + lax.dot_general(
            col_grad, right_share, (((0,), (1,)), ((), ())), preferred_element_type=jnp.float32
        )
    ).astype(jnp.bfloat16)
    embed_share = lax.dynamic_slice_in_dim(embedding, share_start, share, 1)
    left_part = lax.dot_general(
        embed_share, row_grad, (((0,), (1,)), ((), ())), preferred_element_type=jnp.float32
    )
    right_part = lax.dot_general(
        embed_share, col_grad, (((0,), (1,)), ((), ())), preferred_element_type=jnp.float32
    )
    left_sum, right_sum = lax.psum((left_part, right_part), "rows")
    grad_left, grad_right = (
        lax.all_gather(left_sum, "band", axis=0, tiled=True),
        lax.all_gather(right_sum, "band", axis=0, tiled=True),
    )
    return (
        predicted,
        grad_embedding,
        grad_left,
        grad_right,
        grad_in,
        grad_out,
        grad_head,
        grad_bias,
    )


def solution(mesh):
    placed = (
        P("rows", None),
        P(),
        P(),
        P(),
        P(),
        P(),
        P(),
        P("rows", "band"),
        P("rows"),
        P("rows", "band", None, None),
    )
    return jax.shard_map(
        on_device,
        mesh=mesh,
        in_specs=placed,
        out_specs=(P("rows", "band", None, None), P("rows", "band"), P(), P(), P(), P(), P(), P()),
        check_vma=False,
    )
```

profile of v0, /device:TPU:0, one launch (start us, length us, event | category | flops | bytes accessed | tf_op | source)
XLA Modules:
  0.0 160.9 jit_solution(8311720177533387643)
XLA Ops:
  2.4 1.3 collective-permute-start
  3.7 1.3 collective-permute-start.1
  5.7 1.3 collective-permute-start.3
  7.0 1.3 collective-permute-start.4
  8.3 1.3 collective-permute-start.5
  12.8 1.3 collective-permute-start.2
  14.1 2.7 %collective-permute-done.4 = bf16[128]{0:T(256)(128)(2,1)S(1)} collective-permute-done((bf16[128]{0:T(256)(128)(2,1)S(1)}, bf16[128]{0:T(256)(128)(2,1)S(1)}, u32[]{:S(2)}, u32[]{:S(2)}) %collective-permute-start.4) | collective-permute-done | bytes 288 | tf_op jit(solution)/shard_map/ppermute | solution.py:13
  16.8 3.4 %collective-permute-done.5 = bf16[128]{0:T(256)(128)(2,1)S(1)} collective-permute-done((bf16[128]{0:T(256)(128)(2,1)S(1)}, bf16[128]{0:T(256)(128)(2,1)S(1)}, u32[]{:S(2)}, u32[]{:S(2)}) %collective-permute-start.5) | collective-permute-done | bytes 288 | tf_op jit(solution)/shard_map/ppermute | solution.py:13
  20.3 4.3 %collective-permute-done.2 = bf16[32,128]{1,0:T(8,128)(2,1)S(1)} collective-permute-done((bf16[32,128]{1,0:T(8,128)(2,1)S(1)}, bf16[32,128]{1,0:T(8,128)(2,1)S(1)}, u32[]{:S(2)}, u32[]{:S(2)}) %collective-permute-start.2) | collective-permute-done | bytes 8224 | tf_op jit(solution)/shard_map/ppermute | solution.py:13
  25.2 2.7 %multiply_convert_fusion = (bf16[128,8192]{0,1:T(8,128)(2,1)S(1)}, f32[128,8192]{0,1:T(8,128)S(1)}) fusion(bf16[32,128]{1,0:T(8,128)(2,1)} %param.13, f32[4,8,64,128]{3,2,1,0:T(8,128)S(1)} %bitcast.119, f32[32]{0:T(128)S(1)} %multiply_reduce_fusion), kind=kOutput, calls=%fused_computation.30 | convolution fusion | flops 77070336 | bytes 7348352 | tf_op jit(solution)/shard_map/while/body/eval_jaxpr/dot_general | solution.py:31
  28.0 2.0 %multiply_convert_fusion.1 = (bf16[128,8192]{0,1:T(8,128)(2,1)S(1)}, f32[128,8192]{0,1:T(8,128)S(1)}) fusion(bf16[32,128]{1,0:T(8,128)(2,1)S(1)} %copy-done.2, f32[4,8,64,128]{3,2,1,0:T(8,128)S(1)} %bitcast.122, f32[32]{0:T(128)S(1)} %multiply_reduce_fusion), kind=kOutput, calls=%fused_computation.31 | convolution fusion | flops 77070336 | bytes 7348352 | tf_op jit(solution)/shard_map/while/body/eval_jaxpr/dot_general | solution.py:31
  33.9 3.7 %fusion.10 = bf16[128,8192]{0,1:T(8,128)(2,1)S(1)} fusion(f32[128,8192]{0,1:T(8,128)S(1)} %get-tuple-element.81, bf16[128,32]{0,1:T(8,128)(2,1)S(1)} %copy-done.1, f32[8192]{0:T(1024)S(1)} %get-tuple-element.70, f32[32]{0:T(128)S(1)} %copy-done.4), kind=kOutput, calls=%fused_computation.22 | convolution fusion | flops 88604672 | bytes 6332544 | tf_op jit(solution)/shard_map/while/body/eval_jaxpr/dot_general | solution.py:47
  39.3 3.5 %fusion.17 = bf16[128,8192]{0,1:T(8,128)(2,1)S(1)} fusion(f32[128,8192]{0,1:T(8,128)S(1)} %get-tuple-element.83, bf16[128,32]{0,1:T(8,128)(2,1)S(1)} %copy-done.1, f32[8192]{0:T(1024)S(1)} %get-tuple-element.71, f32[32]{0:T(128)S(1)} %copy-done.4), kind=kOutput, calls=%fused_computation.29 | convolution fusion | flops 88604672 | bytes 6332544 | tf_op jit(solution)/shard_map/while/body/eval_jaxpr/dot_general | solution.py:47
  44.4 1.4 convolution_bitcast_fusion.8
  47.7 3.4 %collective-permute-start.6 = (f32[32,128]{1,0:T(8,128)S(1)}, f32[32,128]{1,0:T(8,128)S(1)}, u32[]{:S(2)}, u32[]{:S(2)}) collective-permute-start(f32[32,128]{1,0:T(8,128)S(1)} %get-tuple-element.50), channel_id=1, source_target_pairs={{0,4},{4,8},{8,12},{12,16},{16,20},{20,24},{24,28},{1,5},{5,9},{9,... | collective-permute-start | bytes 49160 | tf_op jit(solution)/shard_map/ppermute | solution.py:13
  51.2 4.8 %collective-permute-start.7 = (f32[32,128]{1,0:T(8,128)S(1)}, f32[32,128]{1,0:T(8,128)S(1)}, u32[]{:S(2)}, u32[]{:S(2)}) collective-permute-start(f32[32,128]{1,0:T(8,128)S(1)} %get-tuple-element.69), channel_id=1, source_target_pairs={{0,8},{4,12},{8,16},{12,20},{16,24},{20,28},{1,9},{5,13},{9,17},{1... | collective-permute-start | bytes 49160 | tf_op jit(solution)/shard_map/ppermute | solution.py:13
  55.9 2.0 %collective-permute-start.8 = (f32[32,128]{1,0:T(8,128)S(1)}, f32[32,128]{1,0:T(8,128)S(1)}, u32[]{:S(2)}, u32[]{:S(2)}) collective-permute-start(f32[32,128]{1,0:T(8,128)S(1)} %get-tuple-element.68), channel_id=1, source_target_pairs={{0,12},{4,16},{8,20},{12,24},{16,28},{1,13},{5,17},{9,21},{13,25},... | collective-permute-start | bytes 49160 | tf_op jit(solution)/shard_map/ppermute | solution.py:13
  58.6 1.6 fusion.19
  60.9 39.1 %all-reduce = (f32[32,128]{1,0:T(8,128)}, f32[128,32]{0,1:T(8,128)}, f32[32]{0:T(128)}, f32[32,4]{0,1:T(4,128)}) all-reduce(f32[32,128]{1,0:T(8,128)S(1)} %convolution_add_fusion.2, f32[128,32]{0,1:T(8,128)S(1)} %convolution_add_fusion.1, f32[32]{0:T(128)S(1)} %fusion.19, ...), channel_id=1, replica_groups=mesh['rows'=8,'band'=4] {'rows','band'}, use_global_device_ids=true, to_apply=%region_9.10 | all-reduce | flops 8352 | bytes 66816 | tf_op jit(solution)/shard_map/psum | solution.py:194
  100.1 10.3 %all-reduce.2 = (bf16[32,128]{1,0:T(8,128)(2,1)S(1)}, bf16[32,128]{1,0:T(8,128)(2,1)S(1)}) all-reduce(f32[32,128]{1,0:T(8,128)S(1)} %pad_maximum_fusion.1, f32[32,128]{1,0:T(8,128)S(1)} %fusion.40), channel_id=1, replica_groups=mesh['rows'=8,'band'=4] {'band'}, use_global_device_ids=true, to_apply=%region_3.4 | all-reduce | flops 8192 | bytes 49152 | tf_op jit(solution)/shard_map/psum | solution.py:191
  111.5 36.1 %all-reduce.1 = (f32[128,32]{0,1:T(8,128)S(1)}, f32[128,32]{0,1:T(8,128)S(1)}) all-reduce(f32[128,32]{0,1:T(8,128)S(1)} %fusion.35, f32[128,32]{0,1:T(8,128)S(1)} %fusion.37), channel_id=1, replica_groups=mesh['rows'=8,'band'=4] {'rows'}, use_global_device_ids=true, to_apply=%region_7.8 | all-reduce | flops 8192 | bytes 65536 | tf_op jit(solution)/shard_map/psum | solution.py:216
  147.7 5.2 %all_gather.6 = f32[512,32]{0,1:T(8,128)S(1)} all-gather(f32[128,32]{0,1:T(8,128)S(1)} %get-tuple-element.46), channel_id=1, replica_groups=mesh['rows'=8,'band'=4] {'band'}, dimensions={0}, use_global_device_ids=true | all-gather | bytes 81920 | tf_op jit(solution)/shard_map/all_gather | solution.py:218
  152.9 5.2 %all_gather.7 = f32[512,32]{0,1:T(8,128)S(1)} all-gather(f32[128,32]{0,1:T(8,128)S(1)} %get-tuple-element.47), channel_id=1, replica_groups=mesh['rows'=8,'band'=4] {'band'}, dimensions={0}, use_global_device_ids=true | all-gather | bytes 81920 | tf_op jit(solution)/shard_map/all_gather | solution.py:219
  158.1 1.5 fusion.18
  (56 shorter events, 18.6 us)
Async XLA Ops:
  0.6 0.9 copy-start
  2.4 17.9 %collective-permute-start = (bf16[32,128]{1,0:T(8,128)(2,1)S(1)}, bf16[32,128]{1,0:T(8,128)(2,1)S(1)}, u32[]{:S(2)}, u32[]{:S(2)}) collective-permute-start(bf16[32,128]{1,0:T(8,128)(2,1)S(1)} %convolution_convert_fusion), channel_id=1, source_target_pairs={{4,0},{8,4},{12,8},{16,12},{20,16},{24,20},{28,24},{5,1},{9,5},{13... | collective-permute-start | bytes 24584 | tf_op jit(solution)/shard_map/ppermute | solution.py:13
  3.7 16.6 %collective-permute-start.1 = (bf16[32,128]{1,0:T(8,128)(2,1)S(1)}, bf16[32,128]{1,0:T(8,128)(2,1)S(1)}, u32[]{:S(2)}, u32[]{:S(2)}) collective-permute-start(bf16[32,128]{1,0:T(8,128)(2,1)S(1)} %convolution_convert_fusion), channel_id=1, source_target_pairs={{8,0},{12,4},{16,8},{20,12},{24,16},{28,20},{9,1},{13,5},{17,9},{2... | collective-permute-start | bytes 24584 | tf_op jit(solution)/shard_map/ppermute | solution.py:13
  5.7 7.1 %collective-permute-start.3 = (bf16[128]{0:T(256)(128)(2,1)S(1)}, bf16[128]{0:T(256)(128)(2,1)S(1)}, u32[]{:S(2)}, u32[]{:S(2)}) collective-permute-start(bf16[128]{0:T(256)(128)(2,1)S(1)} %convert_element_type.109), channel_id=1, source_target_pairs={{4,0},{8,4},{12,8},{16,12},{20,16},{24,20},{28,24},{5,1},{9,5},{13... | collective-permute-start | bytes 776 | tf_op jit(solution)/shard_map/ppermute | solution.py:13
  7.0 9.8 %collective-permute-start.4 = (bf16[128]{0:T(256)(128)(2,1)S(1)}, bf16[128]{0:T(256)(128)(2,1)S(1)}, u32[]{:S(2)}, u32[]{:S(2)}) collective-permute-start(bf16[128]{0:T(256)(128)(2,1)S(1)} %convert_element_type.109), channel_id=1, source_target_pairs={{8,0},{12,4},{16,8},{20,12},{24,16},{28,20},{9,1},{13,5},{17,9},{2... | collective-permute-start | bytes 776 | tf_op jit(solution)/shard_map/ppermute | solution.py:13
  8.3 11.9 %collective-permute-start.5 = (bf16[128]{0:T(256)(128)(2,1)S(1)}, bf16[128]{0:T(256)(128)(2,1)S(1)}, u32[]{:S(2)}, u32[]{:S(2)}) collective-permute-start(bf16[128]{0:T(256)(128)(2,1)S(1)} %convert_element_type.109), channel_id=1, source_target_pairs={{12,0},{16,4},{20,8},{24,12},{28,16},{13,1},{17,5},{21,9},{25,13},... | collective-permute-start | bytes 776 | tf_op jit(solution)/shard_map/ppermute | solution.py:13
  12.8 11.8 %collective-permute-start.2 = (bf16[32,128]{1,0:T(8,128)(2,1)S(1)}, bf16[32,128]{1,0:T(8,128)(2,1)S(1)}, u32[]{:S(2)}, u32[]{:S(2)}) collective-permute-start(bf16[32,128]{1,0:T(8,128)(2,1)S(1)} %convolution_convert_fusion), channel_id=1, source_target_pairs={{12,0},{16,4},{20,8},{24,12},{28,16},{13,1},{17,5},{21,9},{25,13},... | collective-permute-start | bytes 24584 | tf_op jit(solution)/shard_map/ppermute | solution.py:13
  25.2 2.8 %copy-start.2 = (bf16[32,128]{1,0:T(8,128)(2,1)S(1)}, bf16[32,128]{1,0:T(8,128)(2,1)}, u32[]{:S(2)}) copy-start(bf16[32,128]{1,0:T(8,128)(2,1)} %param.13) | copy-start | bytes 24580
  28.0 2.0 %copy-start.1 = (bf16[128,32]{0,1:T(8,128)(2,1)S(1)}, bf16[128,32]{0,1:T(8,128)(2,1)}, u32[]{:S(2)}) copy-start(bf16[128,32]{0,1:T(8,128)(2,1)} %param.14) | copy-start | bytes 24580
  30.0 2.0 %copy-start.4 = (f32[32]{0:T(128)S(1)}, f32[32]{0:T(128)}, u32[]{:S(2)}) copy-start(f32[32]{0:T(128)} %param.15) | copy-start | bytes 388
  31.0 2.3 %copy-start.3 = (bf16[1,1,128,128]{3,2,1,0:T(8,128)(2,1)S(1)}, bf16[1,1,128,128]{3,2,1,0:T(8,128)(2,1)}, u32[]{:S(2)}) copy-start(bf16[1,1,128,128]{3,2,1,0:T(8,128)(2,1)} %param.19) | copy-start | bytes 98308
  47.7 52.3 %collective-permute-start.6 = (f32[32,128]{1,0:T(8,128)S(1)}, f32[32,128]{1,0:T(8,128)S(1)}, u32[]{:S(2)}, u32[]{:S(2)}) collective-permute-start(f32[32,128]{1,0:T(8,128)S(1)} %get-tuple-element.50), channel_id=1, source_target_pairs={{0,4},{4,8},{8,12},{12,16},{16,20},{20,24},{24,28},{1,5},{5,9},{9,... | collective-permute-start | bytes 49160 | tf_op jit(solution)/shard_map/ppermute | solution.py:13
  51.2 48.9 %collective-permute-start.7 = (f32[32,128]{1,0:T(8,128)S(1)}, f32[32,128]{1,0:T(8,128)S(1)}, u32[]{:S(2)}, u32[]{:S(2)}) collective-permute-start(f32[32,128]{1,0:T(8,128)S(1)} %get-tuple-element.69), channel_id=1, source_target_pairs={{0,8},{4,12},{8,16},{12,20},{16,24},{20,28},{1,9},{5,13},{9,17},{1... | collective-permute-start | bytes 49160 | tf_op jit(solution)/shard_map/ppermute | solution.py:13
  55.9 44.1 %collective-permute-start.8 = (f32[32,128]{1,0:T(8,128)S(1)}, f32[32,128]{1,0:T(8,128)S(1)}, u32[]{:S(2)}, u32[]{:S(2)}) collective-permute-start(f32[32,128]{1,0:T(8,128)S(1)} %get-tuple-element.68), channel_id=1, source_target_pairs={{0,12},{4,16},{8,20},{12,24},{16,28},{1,13},{5,17},{9,21},{13,25},... | collective-permute-start | bytes 49160 | tf_op jit(solution)/shard_map/ppermute | solution.py:13
where the time goes:
time: 162 us; the launch traced here: 161 us
  blocking collectives  96 us (59%)
  matrix products  27 us (17%)
  starting transfers between devices  17.9 us (11%)
  waiting for transfers between devices  11.1 us (7%)
  other arithmetic  4.46 us (3%)
  local copies, waits for them, and re-layouts  2.72 us (2%)
  between operations  1.62 us (1%)
    psum x1, blocking collectives, on_device(): lax.psum((in_part, out_part, head_part, bias_part), ('rows', 'band'))  39.1 us
    psum x1, blocking collectives, on_device(): left_sum, right_sum = lax.psum((left_part, right_part), 'rows')  36.1 us
    ppermute x9, starting transfers between devices, from_behind(): lax.ppermute(value, axis, [(source, source + steps) for source in range(l...  17.9 us
    ppermute x9, waiting for transfers between devices, from_behind(): lax.ppermute(value, axis, [(source, source + steps) for source in range(l...  11.1 us
    psum x1, blocking collectives, on_device(): row_total, col_total = lax.psum((row_acc, col_own), 'band')  10.3 us
    dot_general x2, matrix products, block_terms(): lax.dot_general(w_out, grad_low, (((1,), (0,)), ((), ())), preferred_elem...  7.13 us
    all_gather x1, blocking collectives, on_device(): lax.all_gather(left_sum, 'band', axis=0, tiled=True)  5.22 us
    all_gather x1, blocking collectives, on_device(): lax.all_gather(right_sum, 'band', axis=0, tiled=True)  5.22 us
  transfers between devices with their start and end apart: 9, of which 4 were waited for; matrix products, arithmetic and copies ran while one was open for 3% of the time, Pallas kernels for 0%

commit v1 on v0

--- a/solution.py
+++ b/solution.py
@@ -192,7 +192,7 @@
     row_grad = row_total.astype(jnp.bfloat16)
     col_grad = col_total.astype(jnp.bfloat16)
     grad_in, grad_out, grad_head, grad_bias = lax.psum(
-        (in_part, out_part, head_part, bias_part), ("rows", "band")
+        lax.psum((in_part, out_part, head_part, bias_part), "band"), "rows"
     )
     share = embedding.shape[1] // lax.axis_size("band")
     share_start = lax.axis_index("band") * share

time: 162 us -> 176 us (1.086)
  blocking collectives: 96 us -> 22.9 us
  waiting for transfers between devices: 11.1 us -> 79.1 us
  between operations: 1.62 us -> 15 us
  local copies, waits for them, and re-layouts: 2.72 us -> 7.75 us
    psum x2 -> x0, blocking collectives: 75.2 us -> none  [the longest x1 39.1 us: on_device(): lax.psum((in_part, out_part, head_part, bias_part), ('rows', 'band'))]
    psum x0 -> x1, waiting for transfers between devices: none -> 68 us  [on_device(): left_sum, right_sum = lax.psum((left_part, right_part), 'rows')]
    unnamed x14 -> x18, local copies, waits for them, and re-layouts: 2.56 us -> 7.59 us
  transfers between devices with their start and end apart: 9 -> 10, of which waited for: 4 -> 5; matrix products, arithmetic and copies ran while one was open for 3% -> 4% of each run, Pallas kernels for 0% -> 0%
where the time goes in v1:
time: 176 us; the launch traced here: 175 us
  waiting for transfers between devices  79.1 us (45%)
  matrix products  28.3 us (16%)
  blocking collectives  22.9 us (13%)
  starting transfers between devices  17.9 us (10%)
  between operations  15 us (9%)
  local copies, waits for them, and re-layouts  7.75 us (4%)
  other arithmetic  4.46 us (3%)
    psum x1, waiting for transfers between devices, on_device(): left_sum, right_sum = lax.psum((left_part, right_part), 'rows')  68 us
    ppermute x9, starting transfers between devices, from_behind(): lax.ppermute(value, axis, [(source, source + steps) for source in range(l...  17.9 us
    psum x1, blocking collectives, on_device(): row_total, col_total = lax.psum((row_acc, col_own), 'band')  12 us
    ppermute x9, waiting for transfers between devices, from_behind(): lax.ppermute(value, axis, [(source, source + steps) for source in range(l...  11.1 us
    unnamed x18, local copies, waits for them, and re-layouts  7.59 us
    dot_general x2, matrix products, block_terms(): lax.dot_general(w_out, grad_low, (((1,), (0,)), ((), ())), preferred_elem...  7.12 us
    all_gather x1, blocking collectives, on_device(): lax.all_gather(right_sum, 'band', axis=0, tiled=True)  5.43 us
    all_gather x1, blocking collectives, on_device(): lax.all_gather(left_sum, 'band', axis=0, tiled=True)  5.43 us
  transfers between devices with their start and end apart: 10, of which 5 were waited for; matrix products, arithmetic and copies ran while one was open for 4% of the time, Pallas kernels for 0%

profile of v1, /device:TPU:0, one launch (start us, length us, event | category | flops | bytes accessed | tf_op | source)
XLA Modules:
  0.0 175.4 jit_solution(346986660405215727)
XLA Ops:
  9.0 1.3 collective-permute-start
  10.3 1.3 collective-permute-start.1
  13.5 1.3 collective-permute-start.4
  14.8 1.3 collective-permute-start.5
  19.3 1.3 collective-permute-start.2
  20.6 2.7 %collective-permute-done.4 = bf16[128]{0:T(256)(128)(2,1)S(1)} collective-permute-done((bf16[128]{0:T(256)(128)(2,1)S(1)}, bf16[128]{0:T(256)(128)(2,1)S(1)}, u32[]{:S(2)}, u32[]{:S(2)}) %collective-permute-start.4) | collective-permute-done | bytes 288 | tf_op jit(solution)/shard_map/ppermute | solution.py:13
  23.3 3.4 %collective-permute-done.5 = bf16[128]{0:T(256)(128)(2,1)S(1)} collective-permute-done((bf16[128]{0:T(256)(128)(2,1)S(1)}, bf16[128]{0:T(256)(128)(2,1)S(1)}, u32[]{:S(2)}, u32[]{:S(2)}) %collective-permute-start.5) | collective-permute-done | bytes 288 | tf_op jit(solution)/shard_map/ppermute | solution.py:13
  26.9 4.3 %collective-permute-done.2 = bf16[32,128]{1,0:T(8,128)(2,1)S(1)} collective-permute-done((bf16[32,128]{1,0:T(8,128)(2,1)S(1)}, bf16[32,128]{1,0:T(8,128)(2,1)S(1)}, u32[]{:S(2)}, u32[]{:S(2)}) %collective-permute-start.2) | collective-permute-done | bytes 8224 | tf_op jit(solution)/shard_map/ppermute | solution.py:13
  31.8 2.7 %multiply_convert_fusion = (bf16[128,8192]{0,1:T(8,128)(2,1)S(1)}, f32[128,8192]{0,1:T(8,128)S(1)}) fusion(bf16[32,128]{1,0:T(8,128)(2,1)} %param.13, f32[4,8,64,128]{3,2,1,0:T(8,128)S(1)} %bitcast.119, f32[32]{0:T(128)S(1)} %multiply_reduce_fusion), kind=kOutput, calls=%fused_computation.30 | convolution fusion | flops 77070336 | bytes 7348352 | tf_op jit(solution)/shard_map/while/body/eval_jaxpr/dot_general | solution.py:31
  34.5 2.0 %multiply_convert_fusion.1 = (bf16[128,8192]{0,1:T(8,128)(2,1)S(1)}, f32[128,8192]{0,1:T(8,128)S(1)}) fusion(bf16[32,128]{1,0:T(8,128)(2,1)S(1)} %copy-done.2, f32[4,8,64,128]{3,2,1,0:T(8,128)S(1)} %bitcast.122, f32[32]{0:T(128)S(1)} %multiply_reduce_fusion), kind=kOutput, calls=%fused_computation.31 | convolution fusion | flops 77070336 | bytes 7348352 | tf_op jit(solution)/shard_map/while/body/eval_jaxpr/dot_general | solution.py:31
  40.4 3.7 %fusion.10 = bf16[128,8192]{0,1:T(8,128)(2,1)S(1)} fusion(f32[128,8192]{0,1:T(8,128)S(1)} %get-tuple-element.85, bf16[128,32]{0,1:T(8,128)(2,1)S(1)} %copy-done.1, f32[8192]{0:T(1024)S(1)} %get-tuple-element.74, f32[32]{0:T(128)S(1)} %copy-done.4), kind=kOutput, calls=%fused_computation.22 | convolution fusion | flops 88604672 | bytes 6332544 | tf_op jit(solution)/shard_map/while/body/eval_jaxpr/dot_general | solution.py:47
  45.9 3.5 %fusion.17 = bf16[128,8192]{0,1:T(8,128)(2,1)S(1)} fusion(f32[128,8192]{0,1:T(8,128)S(1)} %get-tuple-element.87, bf16[128,32]{0,1:T(8,128)(2,1)S(1)} %copy-done.1, f32[8192]{0:T(1024)S(1)} %get-tuple-element.75, f32[32]{0:T(128)S(1)} %copy-done.4), kind=kOutput, calls=%fused_computation.29 | convolution fusion | flops 88604672 | bytes 6332544 | tf_op jit(solution)/shard_map/while/body/eval_jaxpr/dot_general | solution.py:47
  50.9 1.4 convolution_bitcast_fusion.8
  54.3 3.4 %collective-permute-start.6 = (f32[32,128]{1,0:T(8,128)S(1)}, f32[32,128]{1,0:T(8,128)S(1)}, u32[]{:S(2)}, u32[]{:S(2)}) collective-permute-start(f32[32,128]{1,0:T(8,128)S(1)} %get-tuple-element.71), channel_id=1, source_target_pairs={{0,4},{4,8},{8,12},{12,16},{16,20},{20,24},{24,28},{1,5},{5,9},{9,... | collective-permute-start | bytes 49160 | tf_op jit(solution)/shard_map/ppermute | solution.py:13
  57.7 4.8 %collective-permute-start.7 = (f32[32,128]{1,0:T(8,128)S(1)}, f32[32,128]{1,0:T(8,128)S(1)}, u32[]{:S(2)}, u32[]{:S(2)}) collective-permute-start(f32[32,128]{1,0:T(8,128)S(1)} %get-tuple-element.73), channel_id=1, source_target_pairs={{0,8},{4,12},{8,16},{12,20},{16,24},{20,28},{1,9},{5,13},{9,17},{1... | collective-permute-start | bytes 49160 | tf_op jit(solution)/shard_map/ppermute | solution.py:13
  62.5 2.0 %collective-permute-start.8 = (f32[32,128]{1,0:T(8,128)S(1)}, f32[32,128]{1,0:T(8,128)S(1)}, u32[]{:S(2)}, u32[]{:S(2)}) collective-permute-start(f32[32,128]{1,0:T(8,128)S(1)} %get-tuple-element.72), channel_id=1, source_target_pairs={{0,12},{4,16},{8,20},{12,24},{16,28},{1,13},{5,17},{9,21},{13,25},... | collective-permute-start | bytes 49160 | tf_op jit(solution)/shard_map/ppermute | solution.py:13
  65.1 1.6 fusion.19
  67.5 12.0 %all-reduce.1 = (bf16[32,128]{1,0:T(8,128)(2,1)S(1)}, bf16[32,128]{1,0:T(8,128)(2,1)S(1)}, f32[32,128]{1,0:T(8,128)}, f32[128,32]{0,1:T(8,128)}, f32[32]{0:T(128)}, /*index=5*/f32[32,4]{0,1:T(4,128)}) all-reduce(f32[32,128]{1,0:T(8,128)S(1)} %pad_maximum_fusion.1, ...), channel_id=1, replica_groups=mesh['rows'=8,'band'=4] {'band'}, use_global_device_ids=true, to_apply=%region_3.4 | all-reduce | flops 16544 | bytes 115968 | tf_op jit(solution)/shard_map/psum | solution.py:191
  81.9 1.5 fusion.18
  83.4 68.0 %all-reduce.4.cloned.1.call-done = (f32[128,32]{0,1:T(8,128)}, f32[128,32]{0,1:T(8,128)}, f32[32,128]{1,0:T(8,128)}, f32[128,32]{0,1:T(8,128)}, f32[32]{0:T(128)}, /*index=5*/f32[32,4]{0,1:T(4,128)}) async-done(((f32[128,32]{0,1:T(8,128)}, f32[128,32]{0,1:T(8,128)}, f32[32,128]{1,0:T(8,128)}, f32[128,32]{0,1:T(8,128)}, f32[32]{0:T(128)}, /*index=5*/f32[32,4]{0,1:T(4,128)}), (f32[128,32]{0,1:T(8,128)}, ...) | async-done | bytes 66192 | tf_op jit(solution)/shard_map/psum | solution.py:216
  151.3 5.4 %all_gather.6 = f32[512,32]{0,1:T(8,128)S(1)} all-gather(f32[128,32]{0,1:T(8,128)} %get-tuple-element.42), channel_id=1, replica_groups=mesh['rows'=8,'band'=4] {'band'}, dimensions={0}, use_global_device_ids=true | all-gather | bytes 81920 | tf_op jit(solution)/shard_map/all_gather | solution.py:218
  156.8 5.4 %all_gather.7 = f32[512,32]{0,1:T(8,128)S(1)} all-gather(f32[128,32]{0,1:T(8,128)} %get-tuple-element.43), channel_id=1, replica_groups=mesh['rows'=8,'band'=4] {'band'}, dimensions={0}, use_global_device_ids=true | all-gather | bytes 81920 | tf_op jit(solution)/shard_map/all_gather | solution.py:219
  163.5 1.3 copy.52
  164.8 1.3 copy.53
  (61 shorter events, 23.5 us)
Async XLA Ops:
  7.2 0.9 copy-start
  7.2 144.2 %all-reduce.4.cloned.1.call-start = ((), (), s32[]{:S(2)}) async-start(), calls=%async_computation | async-start | bytes 136192 | tf_op jit(solution)/shard_map/psum | solution.py:216
  9.0 17.9 %collective-permute-start = (bf16[32,128]{1,0:T(8,128)(2,1)S(1)}, bf16[32,128]{1,0:T(8,128)(2,1)S(1)}, u32[]{:S(2)}, u32[]{:S(2)}) collective-permute-start(bf16[32,128]{1,0:T(8,128)(2,1)S(1)} %convolution_convert_fusion), channel_id=1, source_target_pairs={{4,0},{8,4},{12,8},{16,12},{20,16},{24,20},{28,24},{5,1},{9,5},{13... | collective-permute-start | bytes 24584 | tf_op jit(solution)/shard_map/ppermute | solution.py:13
  10.3 16.6 %collective-permute-start.1 = (bf16[32,128]{1,0:T(8,128)(2,1)S(1)}, bf16[32,128]{1,0:T(8,128)(2,1)S(1)}, u32[]{:S(2)}, u32[]{:S(2)}) collective-permute-start(bf16[32,128]{1,0:T(8,128)(2,1)S(1)} %convolution_convert_fusion), channel_id=1, source_target_pairs={{8,0},{12,4},{16,8},{20,12},{24,16},{28,20},{9,1},{13,5},{17,9},{2... | collective-permute-start | bytes 24584 | tf_op jit(solution)/shard_map/ppermute | solution.py:13
  12.2 7.1 %collective-permute-start.3 = (bf16[128]{0:T(256)(128)(2,1)S(1)}, bf16[128]{0:T(256)(128)(2,1)S(1)}, u32[]{:S(2)}, u32[]{:S(2)}) collective-permute-start(bf16[128]{0:T(256)(128)(2,1)S(1)} %convert_element_type.109), channel_id=1, source_target_pairs={{4,0},{8,4},{12,8},{16,12},{20,16},{24,20},{28,24},{5,1},{9,5},{13... | collective-permute-start | bytes 776 | tf_op jit(solution)/shard_map/ppermute | solution.py:13
  13.5 9.8 %collective-permute-start.4 = (bf16[128]{0:T(256)(128)(2,1)S(1)}, bf16[128]{0:T(256)(128)(2,1)S(1)}, u32[]{:S(2)}, u32[]{:S(2)}) collective-permute-start(bf16[128]{0:T(256)(128)(2,1)S(1)} %convert_element_type.109), channel_id=1, source_target_pairs={{8,0},{12,4},{16,8},{20,12},{24,16},{28,20},{9,1},{13,5},{17,9},{2... | collective-permute-start | bytes 776 | tf_op jit(solution)/shard_map/ppermute | solution.py:13
  14.8 11.9 %collective-permute-start.5 = (bf16[128]{0:T(256)(128)(2,1)S(1)}, bf16[128]{0:T(256)(128)(2,1)S(1)}, u32[]{:S(2)}, u32[]{:S(2)}) collective-permute-start(bf16[128]{0:T(256)(128)(2,1)S(1)} %convert_element_type.109), channel_id=1, source_target_pairs={{12,0},{16,4},{20,8},{24,12},{28,16},{13,1},{17,5},{21,9},{25,13},... | collective-permute-start | bytes 776 | tf_op jit(solution)/shard_map/ppermute | solution.py:13
  19.3 11.8 %collective-permute-start.2 = (bf16[32,128]{1,0:T(8,128)(2,1)S(1)}, bf16[32,128]{1,0:T(8,128)(2,1)S(1)}, u32[]{:S(2)}, u32[]{:S(2)}) collective-permute-start(bf16[32,128]{1,0:T(8,128)(2,1)S(1)} %convolution_convert_fusion), channel_id=1, source_target_pairs={{12,0},{16,4},{20,8},{24,12},{28,16},{13,1},{17,5},{21,9},{25,13},... | collective-permute-start | bytes 24584 | tf_op jit(solution)/shard_map/ppermute | solution.py:13
  31.7 2.8 %copy-start.2 = (bf16[32,128]{1,0:T(8,128)(2,1)S(1)}, bf16[32,128]{1,0:T(8,128)(2,1)}, u32[]{:S(2)}) copy-start(bf16[32,128]{1,0:T(8,128)(2,1)} %param.13) | copy-start | bytes 24580
  34.5 2.0 %copy-start.1 = (bf16[128,32]{0,1:T(8,128)(2,1)S(1)}, bf16[128,32]{0,1:T(8,128)(2,1)}, u32[]{:S(2)}) copy-start(bf16[128,32]{0,1:T(8,128)(2,1)} %param.14) | copy-start | bytes 24580
  36.5 2.0 %copy-start.4 = (f32[32]{0:T(128)S(1)}, f32[32]{0:T(128)}, u32[]{:S(2)}) copy-start(f32[32]{0:T(128)} %param.15) | copy-start | bytes 388
  37.5 2.3 %copy-start.3 = (bf16[1,1,128,128]{3,2,1,0:T(8,128)(2,1)S(1)}, bf16[1,1,128,128]{3,2,1,0:T(8,128)(2,1)}, u32[]{:S(2)}) copy-start(bf16[1,1,128,128]{3,2,1,0:T(8,128)(2,1)} %param.19) | copy-start | bytes 98308
  54.3 13.2 %collective-permute-start.6 = (f32[32,128]{1,0:T(8,128)S(1)}, f32[32,128]{1,0:T(8,128)S(1)}, u32[]{:S(2)}, u32[]{:S(2)}) collective-permute-start(f32[32,128]{1,0:T(8,128)S(1)} %get-tuple-element.71), channel_id=1, source_target_pairs={{0,4},{4,8},{8,12},{12,16},{16,20},{20,24},{24,28},{1,5},{5,9},{9,... | collective-permute-start | bytes 49160 | tf_op jit(solution)/shard_map/ppermute | solution.py:13
  57.7 9.8 %collective-permute-start.7 = (f32[32,128]{1,0:T(8,128)S(1)}, f32[32,128]{1,0:T(8,128)S(1)}, u32[]{:S(2)}, u32[]{:S(2)}) collective-permute-start(f32[32,128]{1,0:T(8,128)S(1)} %get-tuple-element.73), channel_id=1, source_target_pairs={{0,8},{4,12},{8,16},{12,20},{16,24},{20,28},{1,9},{5,13},{9,17},{1... | collective-permute-start | bytes 49160 | tf_op jit(solution)/shard_map/ppermute | solution.py:13
  62.5 5.0 %collective-permute-start.8 = (f32[32,128]{1,0:T(8,128)S(1)}, f32[32,128]{1,0:T(8,128)S(1)}, u32[]{:S(2)}, u32[]{:S(2)}) collective-permute-start(f32[32,128]{1,0:T(8,128)S(1)} %get-tuple-element.72), channel_id=1, source_target_pairs={{0,12},{4,16},{8,20},{12,24},{16,28},{1,13},{5,17},{9,21},{13,25},... | collective-permute-start | bytes 49160 | tf_op jit(solution)/shard_map/ppermute | solution.py:13
Sparse Core Ops, SparseCore 0:
  82.0 69.3 all-reduce.3
